TPU v7x, 32 devices: a whole 2x2x4 slice. The times are simulated.
32 devices in a mesh: wide: 8 (over z, y), narrow: 4 (over x, core).
Axes of the slice: x: 2, y: 2, z: 4, core: 2. Of those that a mesh axis runs over, the one named last changes fastest.
Arguments:
- left_emb: float32 [8, 256, 256], P('wide', 'narrow'), may hold values from -1.5 to 1.5
- left_acc: float32 [8, 256], P('wide', 'narrow'), may hold values from 0.01 to 1
- right_emb: float32 [8, 256, 256], P('wide', 'narrow'), may hold values from -1.5 to 1.5
- right_acc: float32 [8, 256], P('wide', 'narrow'), may hold values from 0.01 to 1
- operators: float32 [8, 256, 256], replicated, may hold values from -0.375 to 0.375
- op_acc: float32 [8, 256], replicated, may hold values from 10 to 1000
- edge_left: int32 [8, 4, 512], P('wide', 'narrow'), may hold values from 0 to 255
- edge_right: int32 [8, 4, 512], P('wide', 'narrow'), may hold values from 0 to 255
- negatives: int32 [8, 4, 1024], P('wide', 'narrow'), may hold values from 0 to 255
- group_relation: int32 [8, 4], P('wide', 'narrow'), may hold values from 0 to 7
Outputs:
- left_new: float32 [8, 256, 256], P('wide', 'narrow')
- left_acc_new: float32 [8, 256], P('wide', 'narrow')
- right_next: float32 [8, 256, 256], P('wide', 'narrow')
- right_acc_next: float32 [8, 256], P('wide', 'narrow')
- operators_new: float32 [8, 256, 256], replicated
- op_acc_new: float32 [8, 256], replicated
All inputs are finite; a program needn't handle non-finite values.
Results may differ from a plain program's by a relative error of at most 0.0003.
Values sent between devices are 32-bit elements; how exact they have to be, the bound alone decides.
A program may use at most 64 MiB of HBM per device.

v0:
```python
import functools
import jax
import jax.numpy as jnp
from jax import lax
from jax.experimental import pallas as pl
from jax.experimental.pallas import tpu as pltpu
from jax.sharding import PartitionSpec as P

HI = lax.Precision.HIGHEST
MESH = pl.DeviceIdType.MESH
F32 = jnp.float32
BF16 = jnp.bfloat16
VMEM_LIMIT = 32000 * 1024


def from_behind(value, axis, steps):
    count = lax.axis_size(axis)
    pairs = [(source, (source + steps) % count) for source in range(count)]
    return lax.ppermute(value, axis, pairs)


def group_terms(left_rows, right_rows, neg_rows, rel_op):
    t = jnp.dot(left_rows, rel_op, precision=HI)
    pos = jnp.sum(t * right_rows, axis=-1)
    neg = jnp.dot(t, neg_rows.T, precision=HI)
    gpos = -jax.nn.sigmoid(-pos)
    gneg = jax.nn.sigmoid(neg) / neg_rows.shape[0]
    grad_t = gpos[:, None] * right_rows + jnp.dot(gneg, neg_rows, precision=HI)
    grad_left = jnp.dot(grad_t, rel_op.T, precision=HI)
    grad_right = gpos[:, None] * t
    grad_neg = jnp.dot(gneg.T, t, precision=HI)
    grad_op = jnp.dot(left_rows.T, grad_t, precision=HI)
    return (grad_left, grad_right, grad_neg, grad_op)


def adagrad(param, accum, grad):
    accum_new = accum + jnp.mean(grad * grad, axis=-1)
    return (param - 0.1 * grad / (jnp.sqrt(accum_new)[..., None] + 1e-08), accum_new)


def rows_within(terms, ids, count):
    inside = (ids >= 0) & (ids < count)
    target = jnp.where(inside, ids, count)
    return jax.ops.segment_sum(terms, target, num_segments=count + 1)[:count]


def plain_device(
    left_emb,
    left_acc,
    right_emb,
    right_acc,
    operators,
    op_acc,
    edge_left,
    edge_right,
    negatives,
    group_relation,
):
    whole_left, whole_right = (
        lax.all_gather(left_emb, "narrow", axis=1, tiled=True),
        lax.all_gather(right_emb, "narrow", axis=1, tiled=True),
    )
    lid = edge_left[0, 0]
    rid = edge_right[0, 0]
    nid = negatives[0, 0]
    rel = group_relation[0, 0]
    rel_op = lax.dynamic_index_in_dim(operators, rel, 0, keepdims=False)
    dl, dr, dq, dm = group_terms(
        jnp.take(whole_left[0], lid, axis=0),
        jnp.take(whole_right[0], rid, axis=0),
        jnp.take(whole_right[0], nid, axis=0),
        rel_op,
    )
    right_ids = jnp.concatenate([rid, nid], 0)
    right_terms = jnp.concatenate([dr, dq], 0)
    rows = left_emb.shape[1]
    width = left_emb.shape[2]
    grads = lax.psum_scatter(
        jnp.concatenate(
            [
                rows_within(dl, lid, lax.axis_size("narrow") * rows),
                rows_within(right_terms, right_ids, lax.axis_size("narrow") * rows),
            ],
            1,
        ),
        "narrow",
        scatter_dimension=0,
        tiled=True,
    )
    new_left, new_lacc = adagrad(left_emb[0], left_acc[0], grads[:, :width])
    new_right, new_racc = adagrad(right_emb[0], right_acc[0], grads[:, width:])
    pick = (jnp.arange(operators.shape[0], dtype=jnp.int32) == rel).astype(jnp.float32)
    op_term = pick[:, None, None] * dm[None]
    op_total = lax.psum(op_term, ("wide", "narrow"))
    ops_new, opacc_new = adagrad(operators, op_acc, op_total)
    moved_right, moved_racc = from_behind((new_right, new_racc), "wide", lax.axis_size("wide") // 2)
    return (new_left[None], new_lacc[None], moved_right[None], moved_racc[None], ops_new, opacc_new)


def flip(index, d):
    out = 0
    bit = 1
    total = 0
    while bit <= d:
        here = (index // bit) % 2
        if d & bit:
            out = out + (1 - here) * bit
        else:
            out = out + here * bit
        total += bit
        bit *= 2
    return (index // bit) * bit + out if d else index


def halves(a):
    hi = a.astype(BF16)
    return hi, (a - hi.astype(F32)).astype(BF16)


def dot3(a, b, rhs_t=False):
    (ah, al), (bh, bl) = a, b
    dims = (((1,), (1 if rhs_t else 0,)), ((), ()))
    f = lambda u, v: lax.dot_general(u, v, dims, preferred_element_type=F32)
    return f(ah, bh) + (f(ah, bl) + f(al, bh))


def to_column(row):
    n = row.shape[1]
    eye = lax.broadcasted_iota(jnp.int32, (n, n), 0) == lax.broadcasted_iota(jnp.int32, (n, n), 1)
    return jnp.sum(jnp.where(eye, row, 0.0), axis=1, keepdims=True)


def to_row(column):
    n = column.shape[0]
    eye = lax.broadcasted_iota(jnp.int32, (n, n), 0) == lax.broadcasted_iota(jnp.int32, (n, n), 1)
    return jnp.sum(jnp.where(eye, column, 0.0), axis=0, keepdims=True)


def kernel(
    NW,
    NN,
    left,
    lacc_hbm,
    right,
    racc_hbm,
    ops_hbm,
    opacc_hbm,
    lids_hbm,
    rids_hbm,
    nids_hbm,
    rel_ref,
    left_out,
    lacc_out,
    right_out,
    racc_out,
    ops_out,
    opacc_out,
    lacc,
    racc,
    opacc,
    lids,
    rids,
    nids,
    left_v,
    lacc_v,
    racc_v,
    opacc_v,
    ops_v,
    wl,
    wr,
    tag1,
    tag2,
    dm,
    glb,
    grb,
    rs1,
    rl,
    rr,
    rs2,
    part_s,
    part_r,
    agb,
    in_sem,
    res_sem,
    out_sem,
    g_send,
    g_recv,
    t_send,
    t_recv,
    u_send,
    u_recv,
    r_send,
    r_recv,
    s_send,
    s_recv,
    p_send,
    p_recv,
    a_send,
    a_recv,
):
    rows, width = left.shape[1], left.shape[2]
    part = NN * rows
    rels = ops_v.shape[0]
    q = agb.shape[2]
    hr = rels // 2
    NZ = NW // 2
    w = lax.axis_index("wide")
    n = lax.axis_index("narrow")
    z, y = w // 2, w % 2
    x, c = n // 2, n % 2
    sends = []

    def rcopy(src, dst, ss, rs, to_w, to_n):
        cp = pltpu.make_async_remote_copy(
            src_ref=src,
            dst_ref=dst,
            send_sem=ss,
            recv_sem=rs,
            device_id=(to_w, to_n),
            device_id_type=MESH,
        )
        cp.start()
        sends.append(cp)
        return cp

    loads = {}

    def load(name, src, dst):
        cp = pltpu.make_async_copy(src, dst, in_sem.at[len(loads)])
        cp.start()
        loads[name] = cp

    load("l", lids_hbm, lids)
    load("r", rids_hbm, rids)
    load("n", nids_hbm, nids)
    load("left", left.at[0], wl.at[n])
    load("right", right.at[0], wr.at[n])
    load("lacc", lacc_hbm, lacc)
    load("racc", racc_hbm, racc)
    load("opacc", opacc_hbm, opacc)
    load("ops", ops_hbm, ops_v)

    barrier = pltpu.get_barrier_semaphore()
    for d in range(1, NN):
        pl.semaphore_signal(barrier, inc=1, device_id=(w, flip(n, d)), device_id_type=MESH)
    for d in range(1, NW):
        pl.semaphore_signal(barrier, inc=1, device_id=(flip(w, d), n), device_id_type=MESH)
    pl.semaphore_wait(barrier, NN + NW - 2)

    near, far = flip(n, 1), flip(n, 2)
    lfar = rcopy(left.at[0], wl.at[n], g_send.at[0], g_recv.at[0], w, far)
    rfar = rcopy(right.at[0], wr.at[n], g_send.at[1], g_recv.at[1], w, far)
    lnear = rcopy(left.at[0], wl.at[n], g_send.at[2], g_recv.at[2], w, near)
    rnear = rcopy(right.at[0], wr.at[n], g_send.at[3], g_recv.at[3], w, near)
    rel = rel_ref[0, 0]
    tag1[n] = jnp.broadcast_to(rel.astype(F32), tag1.shape[1:])
    tags = [
        rcopy(tag1.at[n], tag1.at[n], t_send.at[d], t_recv.at[d], w, flip(n, d))
        for d in range(1, NN)
    ]

    for name in "lrn":
        loads[name].wait()
    edges, negs = lids.shape[2], nids.shape[2]
    ohl = lax.broadcasted_iota(jnp.int32, (part, edges), 0) == lids[0]
    ohr = lax.broadcasted_iota(jnp.int32, (part, edges), 0) == rids[0]
    ohn = lax.broadcasted_iota(jnp.int32, (part, negs), 0) == nids[0]
    nt = (((1,), (1,)), ((), ()))
    ohl16 = jnp.where(ohl, 1.0, 0.0).astype(BF16)
    ohr16 = jnp.where(ohr, 1.0, 0.0).astype(BF16)
    ohn16 = jnp.where(ohn, 1.0, 0.0).astype(BF16)
    pairs = lax.dot_general(ohl16, ohr16, nt, preferred_element_type=F32)
    cl = jnp.sum(jnp.where(ohl, 1.0, 0.0), axis=1, keepdims=True)
    cn = lax.dot_general(jnp.ones((8, negs), BF16), ohn16, nt, preferred_element_type=F32)[0:1]
    weight = cl * cn

    loads["ops"].wait()
    m = halves(ops_v[rel])

    lfar.wait_recv()
    lfwd = rcopy(wl.at[far], wl.at[far], g_send.at[4], g_recv.at[4], w, near)
    rfar.wait_recv()
    rfwd = rcopy(wr.at[far], wr.at[far], g_send.at[5], g_recv.at[5], w, near)
    for cp in tags:
        cp.wait_recv()
    spot = lax.broadcasted_iota(jnp.int32, tag2.shape[1:], 0)
    packed = jnp.zeros(tag2.shape[1:], F32)
    for k in range(NN):
        packed = packed + jnp.where(spot == k, tag1[k], 0.0)
    tag2[w] = packed
    tags2 = [
        rcopy(tag2.at[w], tag2.at[w], u_send.at[d], u_recv.at[d], flip(w, d), n)
        for d in range(1, NW)
    ]
    loads["left"].wait()
    loads["right"].wait()
    lnear.wait_recv()
    lfwd.wait_recv()
    wl_all = wl[...].reshape(part, width)
    t = dot3(halves(wl_all), m)
    th = halves(t)
    wlt = halves(wl_all.T)
    rnear.wait_recv()
    rfwd.wait_recv()
    wrh = halves(wr[...].reshape(part, width))
    s = dot3(th, wrh, rhs_t=True)
    g = weight * (jax.nn.sigmoid(s) / negs) - pairs * jax.nn.sigmoid(-s)
    dt = halves(dot3(halves(g), wrh))
    dm[...] = dot3(wlt, dt)
    first = []
    for d in range(1, NN):
        to = flip(n, d)
        at = pl.ds(pl.multiple_of(to * rows, rows), rows)
        first.append(rcopy(dm.at[at], rs1.at[n], r_send.at[0, d], r_recv.at[0, d], w, to))
    own = pl.ds(pl.multiple_of(n * rows, rows), rows)
    rs1[n] = dm[own, :]

    grb[...] = dot3(halves(g.T), th)
    right_sends = []
    for d in range(1, NN):
        to = flip(n, d)
        at = pl.ds(pl.multiple_of(to * rows, rows), rows)
        right_sends.append(rcopy(grb.at[at], rr.at[n], r_send.at[1, d], r_recv.at[1, d], w, to))
    for cp in first:
        cp.wait_recv()
    second = []
    for d in range(NW - 1, 0, -1):
        to = flip(w, d)
        at = pl.ds(pl.multiple_of(to * q, q), q)
        second.append(
            rcopy(rs1.at[:, at, :], rs2.at[w], s_send.at[d], s_recv.at[d], to, n)
        )
    rs2[w] = rs1[:, pl.ds(pl.multiple_of(w * q, q), q), :]
    glb[...] = dot3(dt, m, rhs_t=True)
    left_sends = []
    for d in range(1, NN):
        to = flip(n, d)
        at = pl.ds(pl.multiple_of(to * rows, rows), rows)
        left_sends.append(rcopy(glb.at[at], rl.at[n], r_send.at[2, d], r_recv.at[2, d], w, to))

    def row_step(p, acc_row, grad):
        acc = to_column(acc_row) + jnp.sum(grad * grad, axis=1, keepdims=True) / width
        return p - 0.1 * grad / (jnp.sqrt(acc) + 1e-08), to_row(acc)

    gr = grb[own, :]
    for d, cp in zip(range(1, NN), right_sends):
        cp.wait_recv()
        gr = gr + rr[flip(n, d)]
    for name in ("lacc", "racc", "opacc"):
        loads[name].wait()
    new_right, new_racc = row_step(wr[n], racc[...], gr)
    part_s[0:rows, :] = new_right
    part_s[rows : rows + 8, 0:rows] = jnp.broadcast_to(new_racc, (8, rows))
    part_s[rows : rows + 8, rows:width] = jnp.zeros((8, width - rows), F32)
    moved = rcopy(part_s, part_r, p_send, p_recv, (w + NW // 2) % NW, n)

    for cp in tags2:
        cp.wait_recv()
    for cp in second:
        cp.wait_recv()

    which = lax.broadcasted_iota(jnp.int32, (rels, width), 0).astype(F32)

    def add_up(i, total):
        for k in range(NN):
            row = tag2[i, k : k + 1, :]
            row = jnp.concatenate([row] * (width // row.shape[1]), axis=1)
            pick = jnp.where(which == row, 1.0, 0.0)
            total = total + pick[:, None, :] * rs2[i, k][None]
        return total

    gop = lax.fori_loop(0, NW, add_up, jnp.zeros((rels, q, width), F32))
    j = n * NW + w
    mine = pl.ds(pl.multiple_of(j * q, q), q)
    place = lax.broadcasted_iota(jnp.int32, (rels, q, width), 2) == (
        j * q + lax.broadcasted_iota(jnp.int32, (rels, q, width), 1)
    )
    old = jnp.sum(jnp.where(place, opacc[...][:, None, :], 0.0), axis=2, keepdims=True)
    acc = old + jnp.sum(gop * gop, axis=2, keepdims=True) / width
    agb[j, 0] = jnp.sum(jnp.where(place, acc, 0.0), axis=1)
    agb[j, 1 : 1 + rels] = ops_v[:, mine, :] - 0.1 * gop / (jnp.sqrt(acc) + 1e-08)

    def shard(dz, ey, fx, core=c):
        return (flip(x, fx) * 2 + core) * NW + flip(z, dz) * 2 + flip(y, ey)

    def lo(i):
        return agb.at[i, 0 : 1 + hr]

    def hi(i):
        return agb.at[i, 1 + hr : 1 + rels]

    out_lo = lambda i: pltpu.make_async_copy(
        agb.at[i, 1 : 1 + hr],
        ops_out.at[0:hr, pl.ds(pl.multiple_of(i * q, q), q), :],
        out_sem,
    ).start()
    out_hi = lambda i: pltpu.make_async_copy(
        hi(i),
        ops_out.at[hr:rels, pl.ds(pl.multiple_of(i * q, q), q), :],
        out_sem,
    ).start()
    count = [0]

    def pass_on(view, i, to_w, to_n):
        k = count[0]
        count[0] += 1
        return rcopy(view(i), view(i), a_send.at[k], a_recv.at[k], to_w, to_n)

    wy = z * 2 + (1 - y)
    core_lo, core_hi = {}, {}

    def give_lo(dz, ey, fx):
        i = shard(dz, ey, fx)
        core_lo[dz, ey, fx] = pass_on(lo, i, w, near)
        out_lo(i)

    def give_hi(dz, ey, fx):
        i = shard(dz, ey, fx)
        core_hi[dz, ey, fx] = pass_on(hi, i, w, near)
        out_hi(i)

    along_z = {
        dz: pass_on(lambda i: agb.at[i], j, flip(z, dz) * 2 + y, n) for dz in range(1, NZ)
    }
    y_lo = {0: pass_on(lo, j, wy, n)}
    x_hi = {0: pass_on(hi, j, w, far)}
    give_lo(0, 0, 0)
    give_hi(0, 0, 0)
    x_lo, y_hi = {}, {}
    x_lo[0, 0] = pass_on(lo, j, w, far)
    y_hi[0, 0] = pass_on(hi, j, wy, n)
    for dz in range(1, NZ):
        along_z[dz].wait_recv()
        i = shard(dz, 0, 0)
        y_lo[dz] = pass_on(lo, i, wy, n)
        x_hi[dz] = pass_on(hi, i, w, far)
        x_lo[dz, 0] = pass_on(lo, i, w, far)
        y_hi[dz, 0] = pass_on(hi, i, wy, n)
        give_lo(dz, 0, 0)
        give_hi(dz, 0, 0)
    for dz in range(NZ):
        y_lo[dz].wait_recv()
        x_lo[dz, 1] = pass_on(lo, shard(dz, 1, 0), w, far)
        give_lo(dz, 1, 0)
        x_hi[dz].wait_recv()
        y_hi[dz, 1] = pass_on(hi, shard(dz, 0, 1), wy, n)
        give_hi(dz, 0, 1)

    gl = glb[own, :]
    for d, cp in zip(range(1, NN), left_sends):
        cp.wait_recv()
        gl = gl + rl[flip(n, d)]
    new_left, new_lacc = row_step(wl[n], lacc[...], gl)
    left_v[0] = new_left
    lacc_v[...] = new_lacc
    moved.wait_recv()
    racc_v[...] = part_r[rows : rows + 1, 0:rows]
    results = [
        pltpu.make_async_copy(src, dst, res_sem.at[k])
        for k, (src, dst) in enumerate(
            [
                (left_v, left_out),
                (lacc_v, lacc_out),
                (part_r.at[0:rows], right_out.at[0]),
                (racc_v, racc_out),
                (opacc_v, opacc_out),
            ]
        )
    ]
    for cp in results[:4]:
        cp.start()

    for dz in range(NZ):
        for e in range(2):
            x_lo[dz, e].wait_recv()
            give_lo(dz, e, 1)
            y_hi[dz, e].wait_recv()
            give_hi(dz, 1, e)
    for key, cp in core_lo.items():
        cp.wait_recv()
        out_lo(shard(*key, core=1 - c))
    for key, cp in core_hi.items():
        cp.wait_recv()
        out_hi(shard(*key, core=1 - c))
    opacc_v[...] = jnp.sum(agb[:, 0], axis=0)
    results[4].start()
    for cp in results:
        cp.wait()
    for cp in sends:
        cp.wait_send()
    pltpu.make_async_copy(ops_v, ops_out, out_sem).wait()


def write_out(*refs):
    ins, outs, sem = refs[:6], refs[6:12], refs[12]
    moves = [pltpu.make_async_copy(a, b, sem.at[k]) for k, (a, b) in enumerate(zip(ins, outs))]
    moves[4].start()
    for k in (0, 2, 1, 3, 5):
        moves[k].start()
    for cp in moves:
        cp.wait()


def kernel_device(NW, NN, *args):
    left_emb, left_acc, right_emb, right_acc, operators, op_acc = args[:6]
    rows, width = left_emb.shape[1:]
    part = rows * NN
    rels = operators.shape[0]
    q = operators.shape[1] // (NW * NN)
    left_to_compiler = pl.BlockSpec(memory_space=pl.ANY)
    dma = pltpu.SemaphoreType.DMA
    steps = (NW // 2 - 1) + 2 * (NW // 2) + 2 * NW + 4 * NW
    V = lambda *shape: pltpu.VMEM(shape, F32)
    like = lambda a: pltpu.VMEM(a.shape, a.dtype)
    shapes = [jax.ShapeDtypeStruct(a.shape, a.dtype) for a in args[:6]]
    found = pl.pallas_call(
        functools.partial(kernel, NW, NN),
        out_shape=shapes,
        in_specs=[pl.BlockSpec(memory_space=pltpu.HBM)] * 9
        + [pl.BlockSpec(memory_space=pltpu.SMEM)],
        out_specs=[left_to_compiler] * 6,
        scratch_shapes=[
            like(left_acc),
            like(right_acc),
            like(op_acc),
            like(args[6]),
            like(args[7]),
            like(args[8]),
            like(left_emb),
            like(left_acc),
            like(right_acc),
            like(op_acc),
            V(*operators.shape),
            V(NN, rows, width),
            V(NN, rows, width),
            V(NN, 8, 128),
            V(NW, 8, 128),
            V(width, width),
            V(part, width),
            V(part, width),
            V(NN, rows, width),
            V(NN, rows, width),
            V(NN, rows, width),
            V(NW, NN, q, width),
            V(rows + 8, width),
            V(rows + 8, width),
            V(NW * NN, rels + 1, q, width),
            dma((9,)),
            dma((5,)),
            dma,
            dma((6,)),
            dma((6,)),
            dma((NN,)),
            dma((NN,)),
            dma((NW,)),
            dma((NW,)),
            dma((3, NN)),
            dma((3, NN)),
            dma((NW,)),
            dma((NW,)),
            dma,
            dma,
            dma((steps,)),
            dma((steps,)),
        ],
        compiler_params=pltpu.CompilerParams(
            collective_id=0, has_side_effects=True, vmem_limit_bytes=VMEM_LIMIT
        ),
    )(*[pltpu.with_memory_space_constraint(a, pltpu.HBM) for a in args[:9]], args[9])
    return pl.pallas_call(
        write_out,
        out_shape=shapes,
        in_specs=[left_to_compiler] * 6,
        out_specs=[left_to_compiler] * 6,
        scratch_shapes=[dma((6,))],
        compiler_params=pltpu.CompilerParams(vmem_limit_bytes=VMEM_LIMIT),
    )(*found)


def fits(NW, NN, left, ops):
    rows, width = left[1] // NN, left[2]
    devices = NW * NN
    return (
        NN == 4
        and NW >= 4
        and NW & (NW - 1) == 0
        and ops[1] == width
        and ops[1] % (8 * devices) == 0
        and ops[1] // devices == ops[0]
        and ops[1] // NN == rows
        and rows % 8 == 0
        and rows < width
        and width % 128 == 0
    )


def solution(mesh):
    NW, NN = mesh.shape["wide"], mesh.shape["narrow"]
    in_specs = (
        P("wide", "narrow", None),
        P("wide", "narrow"),
        P("wide", "narrow", None),
        P("wide", "narrow"),
        P(),
        P(),
        P("wide", "narrow", None),
        P("wide", "narrow", None),
        P("wide", "narrow", None),
        P("wide", "narrow"),
    )
    out_specs = (
        P("wide", "narrow", None),
        P("wide", "narrow"),
        P("wide", "narrow", None),
        P("wide", "narrow"),
        P(),
        P(),
    )

    def step(*args):
        ok = fits(NW, NN, args[0].shape, args[4].shape)
        body = functools.partial(kernel_device, NW, NN) if ok else plain_device
        return jax.shard_map(
            body, mesh=mesh, in_specs=in_specs, out_specs=out_specs, check_vma=False
        )(*args)

    return step
```

profile of v0, /device:TPU:0, one launch (start us, length us, event | category | flops | bytes accessed | tf_op | source)
XLA Modules:
  0.0 47.8 jit_solution(10017082744791007596)
XLA Ops:
  1.3 45.1 %shard_map.145 = (f32[1,64,256]{2,1,0:T(8,128)S(1)}, f32[1,64]{1,0:T(1,128)S(1)}, f32[1,64,256]{2,1,0:T(8,128)S(1)}, f32[1,64]{1,0:T(1,128)S(1)}, f32[8,256,256]{2,1,0:T(8,128)S(1)}, /*index=5*/f32[8,256]{1,0:T(8,128)S(1)}) custom-call(f32[1,64,256]{2,1,0:T(8,128)} %left.1, f32[1,64]{1,0:T(1,128)} %lacc_hbm.1, f32[1,64,256]{2,1,0:T(8,128)} %right.1, ...), custom_call_target="tpu_custom_call" | custom-call | tf_op jit(solution)/shard_map/pallas_call | solution.py:516
  46.4 1.4 %shard_map.146 = (f32[1,64,256]{2,1,0:T(8,128)}, f32[1,64]{1,0:T(1,128)}, f32[1,64,256]{2,1,0:T(8,128)}, f32[1,64]{1,0:T(1,128)}, f32[8,256,256]{2,1,0:T(8,128)}, /*index=5*/f32[8,256]{1,0:T(8,128)}) custom-call(f32[1,64,256]{2,1,0:T(8,128)S(1)} %get-tuple-element.12.refs_0_, f32[1,64]{1,0:T(1,128)S(1)} %get-tuple-element.13.refs_1_, ...), custom_call_target="tpu_custom_call" | custom-call | tf_op jit(solution)/shard_map/pallas_call | solution.py:570
where the time goes:
time: 48.2 us; the launch traced here: 47.8 us
  Pallas kernels  46.5 us (96%)
  between operations  1.29 us (3%)
    pallas_call x1, Pallas kernels, kernel_device(): pl.pallas_call(functools.partial(kernel, NW, NN), out_shape=shapes, in_sp...  45.1 us
    pallas_call x1, Pallas kernels, kernel_device(): pl.pallas_call(write_out, out_shape=shapes, in_specs=[left_to_compiler] *...  1.4 us

commit v1 on v0

--- a/solution.py
+++ b/solution.py
@@ -11,6 +11,7 @@
 F32 = jnp.float32
 BF16 = jnp.bfloat16
 VMEM_LIMIT = 32000 * 1024
+LANES = 128
 
 
 def from_behind(value, axis, steps):
@@ -168,47 +169,54 @@
     ops_v,
     wl,
     wr,
-    tag1,
-    tag2,
+    tagb,
+    accb,
     dm,
     glb,
     grb,
-    rs1,
-    rl,
-    rr,
-    rs2,
+    near_l,
+    near_r,
+    far_ls,
+    far_rs,
+    far_l,
+    far_r,
+    rsb,
     part_s,
     part_r,
-    agb,
+    own_v,
     in_sem,
     res_sem,
     out_sem,
+    here_sem,
     g_send,
     g_recv,
     t_send,
     t_recv,
-    u_send,
-    u_recv,
-    r_send,
-    r_recv,
     s_send,
     s_recv,
+    q_send,
+    q_recv,
     p_send,
     p_recv,
+    c_send,
+    c_recv,
     a_send,
     a_recv,
 ):
     rows, width = left.shape[1], left.shape[2]
     part = NN * rows
     rels = ops_v.shape[0]
-    q = agb.shape[2]
+    q = own_v.shape[1]
     hr = rels // 2
     NZ = NW // 2
+    devices = NW * NN
+    lanes = accb.shape[2]
     w = lax.axis_index("wide")
     n = lax.axis_index("narrow")
     z, y = w // 2, w % 2
     x, c = n // 2, n % 2
-    sends = []
+    j = n * NW + w
+    near, far = flip(n, 1), flip(n, 2)
 
     def rcopy(src, dst, ss, rs, to_w, to_n):
         cp = pltpu.make_async_remote_copy(
@@ -220,8 +228,10 @@
             device_id_type=MESH,
         )
         cp.start()
-        sends.append(cp)
         return cp
+
+    def take(ref, sem):
+        pltpu.make_async_copy(ref, ref, sem).wait()
 
     loads = {}
 
@@ -247,17 +257,12 @@
         pl.semaphore_signal(barrier, inc=1, device_id=(flip(w, d), n), device_id_type=MESH)
     pl.semaphore_wait(barrier, NN + NW - 2)
 
-    near, far = flip(n, 1), flip(n, 2)
-    lfar = rcopy(left.at[0], wl.at[n], g_send.at[0], g_recv.at[0], w, far)
-    rfar = rcopy(right.at[0], wr.at[n], g_send.at[1], g_recv.at[1], w, far)
-    lnear = rcopy(left.at[0], wl.at[n], g_send.at[2], g_recv.at[2], w, near)
-    rnear = rcopy(right.at[0], wr.at[n], g_send.at[3], g_recv.at[3], w, near)
-    rel = rel_ref[0, 0]
-    tag1[n] = jnp.broadcast_to(rel.astype(F32), tag1.shape[1:])
-    tags = [
-        rcopy(tag1.at[n], tag1.at[n], t_send.at[d], t_recv.at[d], w, flip(n, d))
-        for d in range(1, NN)
-    ]
+    rcopy(left.at[0], wl.at[n], g_send, g_recv.at[0], w, far)
+    rcopy(right.at[0], wr.at[n], g_send, g_recv.at[1], w, far)
+    rcopy(left.at[0], wl.at[n], g_send, g_recv.at[2], w, near)
+    rcopy(right.at[0], wr.at[n], g_send, g_recv.at[3], w, near)
+    for d in range(1, NN):
+        pl.semaphore_signal(here_sem, inc=1, device_id=(w, flip(n, d)), device_id_type=MESH)
 
     for name in "lrn":
         loads[name].wait()
@@ -275,186 +280,175 @@
     weight = cl * cn
 
     loads["ops"].wait()
+    rel = rel_ref[0, 0]
     m = halves(ops_v[rel])
-
-    lfar.wait_recv()
-    lfwd = rcopy(wl.at[far], wl.at[far], g_send.at[4], g_recv.at[4], w, near)
-    rfar.wait_recv()
-    rfwd = rcopy(wr.at[far], wr.at[far], g_send.at[5], g_recv.at[5], w, near)
-    for cp in tags:
-        cp.wait_recv()
-    spot = lax.broadcasted_iota(jnp.int32, tag2.shape[1:], 0)
-    packed = jnp.zeros(tag2.shape[1:], F32)
-    for k in range(NN):
-        packed = packed + jnp.where(spot == k, tag1[k], 0.0)
-    tag2[w] = packed
-    tags2 = [
-        rcopy(tag2.at[w], tag2.at[w], u_send.at[d], u_recv.at[d], flip(w, d), n)
-        for d in range(1, NW)
+    tagb[j] = jnp.broadcast_to(rel.astype(F32), tagb.shape[1:])
+    pl.semaphore_wait(here_sem, NN - 1)
+
+    order = list(range(NZ - 1, 0, -1)) + [0]
+    peers = [
+        (dz, dy, dn)
+        for dz in order
+        for dn in range(NN - 1, -1, -1)
+        for dy in (1, 0)
+        if dz or dy or dn
     ]
+
+    def peer(dz, dy, dn):
+        return flip(z, dz) * 2 + flip(y, dy), flip(n, dn)
+
+    for p in peers:
+        rcopy(tagb.at[j], tagb.at[j], t_send, t_recv, *peer(*p))
+
+    take(wl.at[n], g_recv.at[0])
+    rcopy(wl.at[far], wl.at[far], g_send, g_recv.at[4], w, near)
+    take(wr.at[n], g_recv.at[1])
+    rcopy(wr.at[far], wr.at[far], g_send, g_recv.at[5], w, near)
     loads["left"].wait()
     loads["right"].wait()
-    lnear.wait_recv()
-    lfwd.wait_recv()
+    take(wl.at[n], g_recv.at[2])
+    take(wl.at[n], g_recv.at[4])
     wl_all = wl[...].reshape(part, width)
     t = dot3(halves(wl_all), m)
     th = halves(t)
     wlt = halves(wl_all.T)
-    rnear.wait_recv()
-    rfwd.wait_recv()
+    take(wr.at[n], g_recv.at[3])
+    take(wr.at[n], g_recv.at[5])
     wrh = halves(wr[...].reshape(part, width))
     s = dot3(th, wrh, rhs_t=True)
     g = weight * (jax.nn.sigmoid(s) / negs) - pairs * jax.nn.sigmoid(-s)
     dt = halves(dot3(halves(g), wrh))
     dm[...] = dot3(wlt, dt)
-    first = []
-    for d in range(1, NN):
-        to = flip(n, d)
-        at = pl.ds(pl.multiple_of(to * rows, rows), rows)
-        first.append(rcopy(dm.at[at], rs1.at[n], r_send.at[0, d], r_recv.at[0, d], w, to))
-    own = pl.ds(pl.multiple_of(n * rows, rows), rows)
-    rs1[n] = dm[own, :]
+
+    def slot(i, size):
+        return pl.ds(pl.multiple_of(i * size, size), size)
+
+    for dz, dy, dn in peers:
+        to_w, to_n = peer(dz, dy, dn)
+        rcopy(dm.at[slot(to_n * NW + to_w, q)], rsb.at[j], s_send, s_recv.at[dz], to_w, to_n)
+    rsb[j] = dm[slot(j, q), :]
 
     grb[...] = dot3(halves(g.T), th)
-    right_sends = []
-    for d in range(1, NN):
-        to = flip(n, d)
-        at = pl.ds(pl.multiple_of(to * rows, rows), rows)
-        right_sends.append(rcopy(grb.at[at], rr.at[n], r_send.at[1, d], r_recv.at[1, d], w, to))
-    for cp in first:
-        cp.wait_recv()
-    second = []
-    for d in range(NW - 1, 0, -1):
-        to = flip(w, d)
-        at = pl.ds(pl.multiple_of(to * q, q), q)
-        second.append(
-            rcopy(rs1.at[:, at, :], rs2.at[w], s_send.at[d], s_recv.at[d], to, n)
-        )
-    rs2[w] = rs1[:, pl.ds(pl.multiple_of(w * q, q), q), :]
+    for k in range(2):
+        rcopy(grb.at[slot(k * 2 + 1 - c, rows)], near_r.at[k], q_send, q_recv.at[0], w, near)
     glb[...] = dot3(dt, m, rhs_t=True)
-    left_sends = []
-    for d in range(1, NN):
-        to = flip(n, d)
-        at = pl.ds(pl.multiple_of(to * rows, rows), rows)
-        left_sends.append(rcopy(glb.at[at], rl.at[n], r_send.at[2, d], r_recv.at[2, d], w, to))
+    for k in range(2):
+        rcopy(glb.at[slot(k * 2 + 1 - c, rows)], near_l.at[k], q_send, q_recv.at[1], w, near)
+
+    take(near_r, q_recv.at[0])
+    far_rs[...] = grb[slot((1 - x) * 2 + c, rows), :] + near_r[1 - x]
+    rcopy(far_rs, far_r, q_send, q_recv.at[2], w, far)
+    take(near_l, q_recv.at[1])
+    far_ls[...] = glb[slot((1 - x) * 2 + c, rows), :] + near_l[1 - x]
+    rcopy(far_ls, far_l, q_send, q_recv.at[3], w, far)
 
     def row_step(p, acc_row, grad):
         acc = to_column(acc_row) + jnp.sum(grad * grad, axis=1, keepdims=True) / width
         return p - 0.1 * grad / (jnp.sqrt(acc) + 1e-08), to_row(acc)
 
-    gr = grb[own, :]
-    for d, cp in zip(range(1, NN), right_sends):
-        cp.wait_recv()
-        gr = gr + rr[flip(n, d)]
+    own = slot(n, rows)
     for name in ("lacc", "racc", "opacc"):
         loads[name].wait()
-    new_right, new_racc = row_step(wr[n], racc[...], gr)
+    place = lax.broadcasted_iota(jnp.int32, (rels, q, width), 2) == (
+        j * q + lax.broadcasted_iota(jnp.int32, (rels, q, width), 1)
+    )
+    old = jnp.sum(jnp.where(place, opacc[...][:, None, :], 0.0), axis=2, keepdims=True)
+
+    take(tagb.at[0 : devices - 1], t_recv)
+
+    def add_up(dz, total):
+        for dn in range(NN):
+            for dy in range(2):
+                src_w, src_n = peer(dz, dy, dn)
+                i = src_n * NW + src_w
+                tag = jnp.broadcast_to(tagb[i], (q, lanes))
+                tag = jnp.concatenate([tag] * (width // lanes), axis=1)
+                term = rsb[i]
+                total = [t + jnp.where(tag == k, term, 0.0) for k, t in enumerate(total)]
+        return total
+
+    total = [jnp.zeros((q, width), F32) for k in range(rels)]
+    take(rsb.at[0 : 2 * NN - 1], s_recv.at[0])
+    total = add_up(0, total)
+    take(rsb.at[0 : 2 * NN], s_recv.at[1])
+    total = add_up(1, total)
+    take(far_r, q_recv.at[2])
+    new_right, new_racc = row_step(wr[n], racc[...], grb[own, :] + near_r[x] + far_r[...])
     part_s[0:rows, :] = new_right
     part_s[rows : rows + 8, 0:rows] = jnp.broadcast_to(new_racc, (8, rows))
     part_s[rows : rows + 8, rows:width] = jnp.zeros((8, width - rows), F32)
     moved = rcopy(part_s, part_r, p_send, p_recv, (w + NW // 2) % NW, n)
-
-    for cp in tags2:
-        cp.wait_recv()
-    for cp in second:
-        cp.wait_recv()
-
-    which = lax.broadcasted_iota(jnp.int32, (rels, width), 0).astype(F32)
-
-    def add_up(i, total):
-        for k in range(NN):
-            row = tag2[i, k : k + 1, :]
-            row = jnp.concatenate([row] * (width // row.shape[1]), axis=1)
-            pick = jnp.where(which == row, 1.0, 0.0)
-            total = total + pick[:, None, :] * rs2[i, k][None]
-        return total
-
-    gop = lax.fori_loop(0, NW, add_up, jnp.zeros((rels, q, width), F32))
-    j = n * NW + w
-    mine = pl.ds(pl.multiple_of(j * q, q), q)
-    place = lax.broadcasted_iota(jnp.int32, (rels, q, width), 2) == (
-        j * q + lax.broadcasted_iota(jnp.int32, (rels, q, width), 1)
-    )
-    old = jnp.sum(jnp.where(place, opacc[...][:, None, :], 0.0), axis=2, keepdims=True)
+    for dz in range(2, NZ):
+        take(rsb.at[0 : 2 * NN], s_recv.at[dz])
+        total = add_up(dz, total)
+
+    gop = jnp.stack(total)
     acc = old + jnp.sum(gop * gop, axis=2, keepdims=True) / width
-    agb[j, 0] = jnp.sum(jnp.where(place, acc, 0.0), axis=1)
-    agb[j, 1 : 1 + rels] = ops_v[:, mine, :] - 0.1 * gop / (jnp.sqrt(acc) + 1e-08)
-
-    def shard(dz, ey, fx, core=c):
-        return (flip(x, fx) * 2 + core) * NW + flip(z, dz) * 2 + flip(y, ey)
-
-    def lo(i):
-        return agb.at[i, 0 : 1 + hr]
-
-    def hi(i):
-        return agb.at[i, 1 + hr : 1 + rels]
-
-    out_lo = lambda i: pltpu.make_async_copy(
-        agb.at[i, 1 : 1 + hr],
-        ops_out.at[0:hr, pl.ds(pl.multiple_of(i * q, q), q), :],
-        out_sem,
-    ).start()
-    out_hi = lambda i: pltpu.make_async_copy(
-        hi(i),
-        ops_out.at[hr:rels, pl.ds(pl.multiple_of(i * q, q), q), :],
-        out_sem,
-    ).start()
-    count = [0]
-
-    def pass_on(view, i, to_w, to_n):
-        k = count[0]
-        count[0] += 1
-        return rcopy(view(i), view(i), a_send.at[k], a_recv.at[k], to_w, to_n)
+    own_v[...] = ops_v[:, slot(j, q), :] - 0.1 * gop / (jnp.sqrt(acc) + 1e-08)
+
+    def at(r0, r1, i):
+        return ops_out.at[r0:r1, slot(i, q), :]
+
+    def shard(zs, ys, xs):
+        return (xs * 2 + c) * NW + zs * 2 + ys
+
+    def away(s):
+        top = z // (NZ // 2)
+        m_z = top * (NZ - 1 - z) + (1 - top) * z
+        v = s + (s - m_z + NZ) // NZ
+        return top * (NZ - 1 - v) + (1 - top) * v
 
     wy = z * 2 + (1 - y)
-    core_lo, core_hi = {}, {}
-
-    def give_lo(dz, ey, fx):
-        i = shard(dz, ey, fx)
-        core_lo[dz, ey, fx] = pass_on(lo, i, w, near)
-        out_lo(i)
-
-    def give_hi(dz, ey, fx):
-        i = shard(dz, ey, fx)
-        core_hi[dz, ey, fx] = pass_on(hi, i, w, near)
-        out_hi(i)
-
-    along_z = {
-        dz: pass_on(lambda i: agb.at[i], j, flip(z, dz) * 2 + y, n) for dz in range(1, NZ)
-    }
-    y_lo = {0: pass_on(lo, j, wy, n)}
-    x_hi = {0: pass_on(hi, j, w, far)}
-    give_lo(0, 0, 0)
-    give_hi(0, 0, 0)
-    x_lo, y_hi = {}, {}
-    x_lo[0, 0] = pass_on(lo, j, w, far)
-    y_hi[0, 0] = pass_on(hi, j, wy, n)
-    for dz in range(1, NZ):
-        along_z[dz].wait_recv()
-        i = shard(dz, 0, 0)
-        y_lo[dz] = pass_on(lo, i, wy, n)
-        x_hi[dz] = pass_on(hi, i, w, far)
-        x_lo[dz, 0] = pass_on(lo, i, w, far)
-        y_hi[dz, 0] = pass_on(hi, i, wy, n)
-        give_lo(dz, 0, 0)
-        give_hi(dz, 0, 0)
-    for dz in range(NZ):
-        y_lo[dz].wait_recv()
-        x_lo[dz, 1] = pass_on(lo, shard(dz, 1, 0), w, far)
-        give_lo(dz, 1, 0)
-        x_hi[dz].wait_recv()
-        y_hi[dz, 1] = pass_on(hi, shard(dz, 0, 1), wy, n)
-        give_hi(dz, 0, 1)
-
-    gl = glb[own, :]
-    for d, cp in zip(range(1, NN), left_sends):
-        cp.wait_recv()
-        gl = gl + rl[flip(n, d)]
-    new_left, new_lacc = row_step(wl[n], lacc[...], gl)
+    zs = [z] + [away(s) for s in range(NZ - 1)]
+
+    def send(src, dst, kind, z_of, to_w, to_n):
+        rcopy(src, dst, a_send, a_recv.at[kind * NZ + z_of], to_w, to_n)
+
+    def give(src, dst):
+        rcopy(src, dst, a_send, a_recv.at[7 * NZ], w, near)
+
+    def spread(src, i, z_of):
+        lo, hi = at(0, hr, i), at(hr, rels, i)
+        send(src.at[0:hr], lo, 1, z_of, wy, n)
+        send(src.at[hr:rels], hi, 2, z_of, w, far)
+        send(src.at[0:hr], lo, 3, z_of, w, far)
+        send(src.at[hr:rels], hi, 4, z_of, wy, n)
+        give(src, at(0, rels, i))
+
+    def pass_on(z_of):
+        lo = at(0, hr, shard(z_of, 1 - y, x))
+        take(lo, a_recv.at[1 * NZ + z_of])
+        send(lo, lo, 5, z_of, w, far)
+        give(lo, lo)
+        hi = at(hr, rels, shard(z_of, y, 1 - x))
+        take(hi, a_recv.at[2 * NZ + z_of])
+        send(hi, hi, 6, z_of, wy, n)
+        give(hi, hi)
+
+    def last(z_of, kind, lo_y):
+        lo = at(0, hr, shard(z_of, lo_y, 1 - x))
+        take(lo, a_recv.at[kind * NZ + z_of])
+        give(lo, lo)
+        hi = at(hr, rels, shard(z_of, 1 - y, x if kind == 3 else 1 - x))
+        take(hi, a_recv.at[(kind + 1) * NZ + z_of])
+        give(hi, hi)
+
+    for s in range(1, NZ):
+        send(own_v, at(0, rels, j), 0, z, zs[s] * 2 + y, n)
+    spread(own_v, j, z)
+    pltpu.make_async_copy(own_v, at(0, rels, j), out_sem).start()
+    k_of = lax.broadcasted_iota(jnp.int32, (rels, q, lanes), 0)
+    r_of = lax.broadcasted_iota(jnp.int32, (rels, q, lanes), 1)
+    lane = lax.broadcasted_iota(jnp.int32, (rels, q, lanes), 2)
+    there = lane == ((k_of + j) * q + r_of) % lanes
+    accb[j] = jnp.sum(jnp.sum(jnp.where(there, acc, 0.0), axis=0), axis=0, keepdims=True)
+    for p in peers:
+        rcopy(accb.at[j], accb.at[j], c_send, c_recv, *peer(*p))
+
+    take(far_l, q_recv.at[3])
+    new_left, new_lacc = row_step(wl[n], lacc[...], glb[own, :] + near_l[x] + far_l[...])
     left_v[0] = new_left
     lacc_v[...] = new_lacc
-    moved.wait_recv()
-    racc_v[...] = part_r[rows : rows + 1, 0:rows]
     results = [
         pltpu.make_async_copy(src, dst, res_sem.at[k])
         for k, (src, dst) in enumerate(
@@ -467,28 +461,52 @@
             ]
         )
     ]
-    for cp in results[:4]:
-        cp.start()
-
-    for dz in range(NZ):
-        for e in range(2):
-            x_lo[dz, e].wait_recv()
-            give_lo(dz, e, 1)
-            y_hi[dz, e].wait_recv()
-            give_hi(dz, 1, e)
-    for key, cp in core_lo.items():
-        cp.wait_recv()
-        out_lo(shard(*key, core=1 - c))
-    for key, cp in core_hi.items():
-        cp.wait_recv()
-        out_hi(shard(*key, core=1 - c))
-    opacc_v[...] = jnp.sum(agb[:, 0], axis=0)
+    results[0].start()
+    results[1].start()
+
+    for s in range(1, NZ):
+        i = shard(zs[s], y, x)
+        take(at(0, rels, i), a_recv.at[zs[s]])
+        spread(at(0, rels, i), i, zs[s])
+        pass_on(zs[s - 1])
+        if s > 1:
+            last(zs[s - 2], 3, y)
+        if s > 2:
+            last(zs[s - 3], 5, 1 - y)
+    pass_on(zs[NZ - 1])
+    take(accb.at[0 : devices - 1], c_recv)
+    groups = lanes // q
+    rest = jnp.concatenate([accb[i] for i in range(devices)], axis=0)
+    diag = lax.broadcasted_iota(jnp.int32, (devices, lanes), 1) // q == (
+        lax.broadcasted_iota(jnp.int32, (devices, lanes), 0) % groups
+    )
+    for k in range(rels):
+        turned = rest if k == 0 else pltpu.roll(rest, lanes - k * q, 1)
+        turned = jnp.where(diag, turned, 0.0)
+        for h in range(devices // groups):
+            opacc_v[k : k + 1, h * lanes : (h + 1) * lanes] = jnp.sum(
+                turned[h * groups : (h + 1) * groups], axis=0, keepdims=True
+            )
     results[4].start()
+    moved.wait_recv()
+    racc_v[...] = part_r[rows : rows + 1, 0:rows]
+    results[2].start()
+    results[3].start()
+    for s in range(max(NZ - 2, 0), NZ):
+        last(zs[s], 3, y)
+    for s in range(max(NZ - 3, 0), NZ):
+        last(zs[s], 5, 1 - y)
+    take(ops_v.at[:, 0 : devices // 2 * q, :], a_recv.at[7 * NZ])
     for cp in results:
         cp.wait()
-    for cp in sends:
-        cp.wait_send()
-    pltpu.make_async_copy(ops_v, ops_out, out_sem).wait()
+    pltpu.make_async_copy(own_v, at(0, rels, j), out_sem).wait()
+    take(ops_v.at[0:2, 0 : 3 * rows, :], g_send)
+    take(ops_v.at[0:2, 0 : 3 * rows, :], q_send)
+    take(tagb.at[0 : devices - 1], t_send)
+    take(accb.at[0 : devices - 1], c_send)
+    take(rsb.at[0 : devices - 1], s_send)
+    moved.wait_send()
+    take(ops_v.at[:, 0 : (devices - 1) * q, :], a_send)
 
 
 def write_out(*refs):
@@ -506,10 +524,11 @@
     rows, width = left_emb.shape[1:]
     part = rows * NN
     rels = operators.shape[0]
-    q = operators.shape[1] // (NW * NN)
+    devices = NW * NN
+    q = operators.shape[1] // devices
+    NZ = NW // 2
     left_to_compiler = pl.BlockSpec(memory_space=pl.ANY)
     dma = pltpu.SemaphoreType.DMA
-    steps = (NW // 2 - 1) + 2 * (NW // 2) + 2 * NW + 4 * NW
     V = lambda *shape: pltpu.VMEM(shape, F32)
     like = lambda a: pltpu.VMEM(a.shape, a.dtype)
     shapes = [jax.ShapeDtypeStruct(a.shape, a.dtype) for a in args[:6]]
@@ -533,35 +552,39 @@
             V(*operators.shape),
             V(NN, rows, width),
             V(NN, rows, width),
-            V(NN, 8, 128),
-            V(NW, 8, 128),
+            V(devices, 1, LANES),
+            V(devices, 1, LANES),
             V(width, width),
             V(part, width),
             V(part, width),
-            V(NN, rows, width),
-            V(NN, rows, width),
-            V(NN, rows, width),
-            V(NW, NN, q, width),
+            V(2, rows, width),
+            V(2, rows, width),
+            V(rows, width),
+            V(rows, width),
+            V(rows, width),
+            V(rows, width),
+            V(devices, q, width),
             V(rows + 8, width),
             V(rows + 8, width),
-            V(NW * NN, rels + 1, q, width),
+            V(rels, q, width),
             dma((9,)),
             dma((5,)),
             dma,
+            pltpu.SemaphoreType.REGULAR,
+            dma,
             dma((6,)),
-            dma((6,)),
-            dma((NN,)),
-            dma((NN,)),
-            dma((NW,)),
-            dma((NW,)),
-            dma((3, NN)),
-            dma((3, NN)),
-            dma((NW,)),
-            dma((NW,)),
-            dma,
-            dma,
-            dma((steps,)),
-            dma((steps,)),
+            dma,
+            dma,
+            dma,
+            dma((NZ,)),
+            dma,
+            dma((4,)),
+            dma,
+            dma,
+            dma,
+            dma,
+            dma,
+            dma((7 * NZ + 1,)),
         ],
         compiler_params=pltpu.CompilerParams(
             collective_id=0, has_side_effects=True, vmem_limit_bytes=VMEM_LIMIT
@@ -590,7 +613,10 @@
         and ops[1] // NN == rows
         and rows % 8 == 0
         and rows < width
-        and width % 128 == 0
+        and width % LANES == 0
+        and ops[0] * ops[0] <= LANES
+        and LANES % ops[0] == 0
+        and devices % (LANES // ops[0]) == 0
     )
 
 

time: 48.2 us -> 41.8 us (0.87)
  Pallas kernels: 46.5 us -> 40.4 us
    pallas_call x1, Pallas kernels: 45.1 us -> 39 us  [kernel_device(): pl.pallas_call(functools.partial(kernel, NW, NN), out_shape=shapes, in_sp...]
where the time goes in v1:
time: 41.8 us; the launch traced here: 41.7 us
  Pallas kernels  40.4 us (97%)
  between operations  1.29 us (3%)
    pallas_call x1, Pallas kernels, kernel_device(): pl.pallas_call(functools.partial(kernel, NW, NN), out_shape=shapes, in_sp...  39 us
    pallas_call x1, Pallas kernels, kernel_device(): pl.pallas_call(write_out, out_shape=shapes, in_specs=[left_to_compiler] *...  1.4 us

profile of v1, /device:TPU:0, one launch (start us, length us, event | category | flops | bytes accessed | tf_op | source)
XLA Modules:
  0.0 41.7 jit_solution(11819872641410889884)
XLA Ops:
  1.3 39.0 %shard_map.145 = (f32[1,64,256]{2,1,0:T(8,128)S(1)}, f32[1,64]{1,0:T(1,128)S(1)}, f32[1,64,256]{2,1,0:T(8,128)S(1)}, f32[1,64]{1,0:T(1,128)S(1)}, f32[8,256,256]{2,1,0:T(8,128)S(1)}, /*index=5*/f32[8,256]{1,0:T(8,128)S(1)}) custom-call(f32[1,64,256]{2,1,0:T(8,128)} %left.1, f32[1,64]{1,0:T(1,128)} %lacc_hbm.1, f32[1,64,256]{2,1,0:T(8,128)} %right.1, ...), custom_call_target="tpu_custom_call" | custom-call | tf_op jit(solution)/shard_map/pallas_call | solution.py:535
  40.3 1.4 %shard_map.146 = (f32[1,64,256]{2,1,0:T(8,128)}, f32[1,64]{1,0:T(1,128)}, f32[1,64,256]{2,1,0:T(8,128)}, f32[1,64]{1,0:T(1,128)}, f32[8,256,256]{2,1,0:T(8,128)}, /*index=5*/f32[8,256]{1,0:T(8,128)}) custom-call(f32[1,64,256]{2,1,0:T(8,128)S(1)} %get-tuple-element.12.refs_0_, f32[1,64]{1,0:T(1,128)S(1)} %get-tuple-element.13.refs_1_, ...), custom_call_target="tpu_custom_call" | custom-call | tf_op jit(solution)/shard_map/pallas_call | solution.py:593

commit v2 on v1

--- a/solution.py
+++ b/solution.py
@@ -377,7 +377,6 @@
     part_s[0:rows, :] = new_right
     part_s[rows : rows + 8, 0:rows] = jnp.broadcast_to(new_racc, (8, rows))
     part_s[rows : rows + 8, rows:width] = jnp.zeros((8, width - rows), F32)
-    moved = rcopy(part_s, part_r, p_send, p_recv, (w + NW // 2) % NW, n)
     for dz in range(2, NZ):
         take(rsb.at[0 : 2 * NN], s_recv.at[dz])
         total = add_up(dz, total)
@@ -468,6 +467,8 @@
         i = shard(zs[s], y, x)
         take(at(0, rels, i), a_recv.at[zs[s]])
         spread(at(0, rels, i), i, zs[s])
+        if s == NZ - 1:
+            moved = rcopy(part_s, part_r, p_send, p_recv, (w + NW // 2) % NW, n)
         pass_on(zs[s - 1])
         if s > 1:
             last(zs[s - 2], 3, y)
@@ -488,14 +489,14 @@
                 turned[h * groups : (h + 1) * groups], axis=0, keepdims=True
             )
     results[4].start()
+    for s in range(max(NZ - 2, 0), NZ):
+        last(zs[s], 3, y)
+    for s in range(max(NZ - 3, 0), NZ):
+        last(zs[s], 5, 1 - y)
     moved.wait_recv()
     racc_v[...] = part_r[rows : rows + 1, 0:rows]
     results[2].start()
     results[3].start()
-    for s in range(max(NZ - 2, 0), NZ):
-        last(zs[s], 3, y)
-    for s in range(max(NZ - 3, 0), NZ):
-        last(zs[s], 5, 1 - y)
     take(ops_v.at[:, 0 : devices // 2 * q, :], a_recv.at[7 * NZ])
     for cp in results:
         cp.wait()

time: 41.8 us -> 38.5 us (0.921)
  Pallas kernels: 40.4 us -> 37.1 us
    pallas_call x1, Pallas kernels: 39 us -> 35.7 us  [kernel_device(): pl.pallas_call(functools.partial(kernel, NW, NN), out_shape=shapes, in_sp...]
where the time goes in v2:
time: 38.5 us; the launch traced here: 38.4 us
  Pallas kernels  37.1 us (96%)
  between operations  1.29 us (3%)
    pallas_call x1, Pallas kernels, kernel_device(): pl.pallas_call(functools.partial(kernel, NW, NN), out_shape=shapes, in_sp...  35.7 us
    pallas_call x1, Pallas kernels, kernel_device(): pl.pallas_call(write_out, out_shape=shapes, in_specs=[left_to_compiler] *...  1.4 us

profile of v2, /device:TPU:0, one launch (start us, length us, event | category | flops | bytes accessed | tf_op | source)
XLA Modules:
  0.0 38.4 jit_solution(1068426909614101347)
XLA Ops:
  1.3 35.7 %shard_map.145 = (f32[1,64,256]{2,1,0:T(8,128)S(1)}, f32[1,64]{1,0:T(1,128)S(1)}, f32[1,64,256]{2,1,0:T(8,128)S(1)}, f32[1,64]{1,0:T(1,128)S(1)}, f32[8,256,256]{2,1,0:T(8,128)S(1)}, /*index=5*/f32[8,256]{1,0:T(8,128)S(1)}) custom-call(f32[1,64,256]{2,1,0:T(8,128)} %left.1, f32[1,64]{1,0:T(1,128)} %lacc_hbm.1, f32[1,64,256]{2,1,0:T(8,128)} %right.1, ...), custom_call_target="tpu_custom_call" | custom-call | tf_op jit(solution)/shard_map/pallas_call | solution.py:536
  36.9 1.4 %shard_map.146 = (f32[1,64,256]{2,1,0:T(8,128)}, f32[1,64]{1,0:T(1,128)}, f32[1,64,256]{2,1,0:T(8,128)}, f32[1,64]{1,0:T(1,128)}, f32[8,256,256]{2,1,0:T(8,128)}, /*index=5*/f32[8,256]{1,0:T(8,128)}) custom-call(f32[1,64,256]{2,1,0:T(8,128)S(1)} %get-tuple-element.12.refs_0_, f32[1,64]{1,0:T(1,128)S(1)} %get-tuple-element.13.refs_1_, ...), custom_call_target="tpu_custom_call" | custom-call | tf_op jit(solution)/shard_map/pallas_call | solution.py:594
